TPU v7x, 128 devices: a whole 4x4x4 slice. The times are simulated.
128 devices in a mesh: strike: 8 (over z, x_hi), normal: 16 (over x_lo, y, core).
Axes of the slice: x: 4 (x_hi: 2, x_lo: 2; x = x_hi * 2 + x_lo), y: 4, z: 4, core: 2. Of those that a mesh axis runs over, the one named last changes fastest.
Arguments:
- velocity: float32 [3, 256, 256, 384], P(None, 'strike', 'normal'), may hold values from -6 to 6
- stress: float32 [6, 256, 256, 384], P(None, 'strike', 'normal'), may hold values from -6 to 6
- modulus: float32 [256, 256, 384], P('strike', 'normal'), may hold values from 0.5 to 2
- buoyancy: float32 [256, 256, 384], P('strike', 'normal'), may hold values from 0.5 to 1.5
- fault_state: float32 [256, 384], P(('strike', 'normal')), may hold values from -0.3 to 0.3
- fault_mask: int32 [256, 384], P(('strike', 'normal')), may hold values 0 or 1
- region_ids: int32 [256, 384], P(('strike', 'normal')), may hold values from 0 to 3
- friction_table: float32 [4, 4], replicated, may hold values from 0.2 to 2
Outputs:
- velocity_out: float32 [3, 256, 256, 384], P(None, 'strike', 'normal')
- stress_out: float32 [6, 256, 256, 384], P(None, 'strike', 'normal')
- slip_rate: float32 [256, 384], P(('strike', 'normal'))
- state_out: float32 [256, 384], P(('strike', 'normal'))
Inputs may be any that keep to these rules, and one draw needn't show every extreme that they name: `region_ids`: region ids index the columns of friction_table.
All inputs are finite; a program needn't handle non-finite values. No bound on the sum of `fault_mask` on one device may be relied on, other than what follows from the above.
Results may differ from a plain program's by a relative error of at most 0.0003.
Values sent between devices are 32-bit elements; how exact they have to be, the bound alone decides.
No kernel may reach another device: no remote copies, remote signals or barrier semaphores. Data moves between devices by JAX's collectives and lax.ppermute only.
A program may use at most 128 MiB of HBM per device.

v0:
```python
import jax
import jax.numpy as jnp
from jax import lax
from jax.sharding import PartitionSpec as P

STEPS = 2
NEWTON = 4
inner_coef = 9.0 / 8.0
outer_coef = -1.0 / 24.0
time_step = 0.1
impedance = 1.0


def with_halo(cells, sides, width):
    for axis, dim in sides:
        count = lax.axis_size(axis)
        ends = count - 1
        head = lax.slice_in_dim(cells, 0, width, axis=dim)
        tail = lax.slice_in_dim(cells, cells.shape[dim] - width, cells.shape[dim], axis=dim)
        cells = jnp.concatenate(
            [
                lax.ppermute(tail, axis, [(i, (i + 1) % count) for i in range(ends)]),
                cells,
                lax.ppermute(head, axis, [((i + 1) % count, i) for i in range(ends)]),
            ],
            axis=dim,
        )
    return cells


def inverse_sinh(values):
    magnitude = jnp.abs(values)
    root = jnp.sqrt(1.0 + magnitude * magnitude)
    result = jnp.log1p(magnitude + magnitude * magnitude / (1.0 + root))
    return jnp.where(values < 0.0, -result, result)


def shifted(padded_values, dimension, offset):
    length = padded_values.shape[dimension] - 4
    return lax.slice_in_dim(padded_values, 2 + offset, 2 + offset + length, axis=dimension)


def forward_diff(padded_values, dimension):
    return inner_coef * (
        shifted(padded_values, dimension, 1) - shifted(padded_values, dimension, 0)
    ) + outer_coef * (shifted(padded_values, dimension, 2) - shifted(padded_values, dimension, -1))


def backward_diff(padded_values, dimension):
    return inner_coef * (
        shifted(padded_values, dimension, 0) - shifted(padded_values, dimension, -1)
    ) + outer_coef * (shifted(padded_values, dimension, 1) - shifted(padded_values, dimension, -2))


def padded(values, dimension):
    widths = [(0, 0)] * values.ndim
    widths[dimension] = (2, 2)
    return jnp.pad(values, widths)


def accelerate(sxx_x, sxy_x, sxz_x, syy_y, sxy_y, syz_y, sxz, syz, szz):
    accel_x = forward_diff(sxx_x, 0) + backward_diff(sxy_y, 1) + backward_diff(padded(sxz, 2), 2)
    accel_y = backward_diff(sxy_x, 0) + forward_diff(syy_y, 1) + backward_diff(padded(syz, 2), 2)
    accel_z = backward_diff(sxz_x, 0) + backward_diff(syz_y, 1) + forward_diff(padded(szz, 2), 2)
    return jnp.stack((accel_x, accel_y, accel_z))


def strain_rates(vx_x, vy_x, vz_x, vx_y, vy_y, vz_y, vel_x, vel_y, vel_z):
    exx = backward_diff(vx_x, 0)
    eyy = backward_diff(vy_y, 1)
    ezz = backward_diff(padded(vel_z, 2), 2)
    trace = exx + eyy + ezz
    rate_xy = forward_diff(vx_y, 1) + forward_diff(vy_x, 0)
    rate_xz = forward_diff(padded(vel_x, 2), 2) + forward_diff(vz_x, 0)
    rate_yz = forward_diff(padded(vel_y, 2), 2) + forward_diff(vz_y, 1)
    return jnp.stack(
        (trace + 2.0 * exx, trace + 2.0 * eyy, trace + 2.0 * ezz, rate_xy, rate_xz, rate_yz)
    )


def lookup(regions, friction_table):
    labels = jnp.arange(friction_table.shape[1], dtype=jnp.float32)
    onehot = (regions[None] == labels[:, None, None]).astype(jnp.float32)
    return jnp.einsum("cr,rxz->cxz", friction_table, onehot, precision=lax.Precision.HIGHEST)


def friction(minus, plus, traction, state_now, mask_now, params):
    direct_effect = params[0]
    evolution_b = params[1]
    inverse_length = params[2]
    normal_stress = params[3]
    locked = traction + impedance * (plus - minus)
    scale_c = 0.5 * jnp.exp(state_now / direct_effect)
    weight = normal_stress * direct_effect
    rate = jnp.zeros_like(locked)
    for newton_step in range(NEWTON):
        argument = scale_c * rate
        residue = locked - impedance * rate - weight * inverse_sinh(argument)
        slope = impedance + weight * scale_c / jnp.sqrt(1.0 + argument * argument)
        rate = rate + residue / slope
    rate = rate * mask_now
    traction_new = locked - impedance * rate
    middle = 0.5 * (minus + plus)
    state_new = state_now + time_step * inverse_length * (
        jnp.exp(-state_now / evolution_b) - jnp.abs(rate)
    )
    return (rate, traction_new, middle - 0.5 * rate, middle + 0.5 * rate, state_new)


def local(velocity, stress, modulus, buoyancy, fault_state, fault_mask, region_ids, friction_table):
    members = lax.axis_size("normal")
    position = lax.axis_index("normal")
    minus_device = position == members // 2 - 1
    plus_device = position == members // 2
    owned_rows = fault_state.shape[0]
    last_row = velocity.shape[2] - 1
    state_now = fault_state
    mask_now = fault_mask.astype(jnp.float32)
    regions = region_ids.astype(jnp.float32)
    params = lookup(regions, friction_table)
    rate = jnp.zeros_like(state_now)
    for time_index in range(STEPS):
        whole_rims = with_halo(stress, (("strike", 1), ("normal", 2)), 2)
        along_x = whole_rims[:, :, 2:-2]
        along_y = whole_rims[:, 2:-2]
        sxx_x, sxy_x, sxz_x = (along_x[0], along_x[3], along_x[4])
        syy_y, sxy_y, syz_y = (along_y[1], along_y[3], along_y[5])
        accel = accelerate(
            sxx_x, sxy_x, sxz_x, syy_y, sxy_y, syz_y, stress[4], stress[5], stress[2]
        )
        velocity = velocity + time_step * buoyancy * accel
        vel_x = velocity[0]
        minus_row = vel_x[:, last_row, :]
        plus_here = vel_x[:, 0, :]
        traction_row = stress[3][:, last_row, :]
        blank = jnp.zeros_like(minus_row)
        contrib = jnp.stack(
            (
                jnp.where(minus_device, minus_row, blank),
                jnp.where(plus_device, plus_here, blank),
                jnp.where(minus_device, traction_row, blank),
            )
        )
        rows_all = lax.psum(contrib, "normal")
        mine = lax.dynamic_slice_in_dim(rows_all, position * owned_rows, owned_rows, 1)
        rate, traction_own, minus_own, plus_own, state_now = friction(
            mine[0], mine[1], mine[2], state_now, mask_now, params
        )
        returned = lax.all_gather(
            jnp.stack((minus_own, plus_own, traction_own)), "normal", axis=1, tiled=True
        )
        minus_full, plus_full, traction_full = (returned[0], returned[1], returned[2])
        new_last = jnp.where(minus_device, minus_full, minus_row)
        new_first = jnp.where(plus_device, plus_full, plus_here)
        vel_x = vel_x.at[:, last_row, :].set(new_last).at[:, 0, :].set(new_first)
        velocity = velocity.at[0].set(vel_x)
        vel_rims = with_halo(velocity, (("strike", 1), ("normal", 2)), 2)
        vel_along_x = vel_rims[:, :, 2:-2]
        vel_along_y = vel_rims[:, 2:-2]
        rates = strain_rates(
            vel_along_x[0],
            vel_along_x[1],
            vel_along_x[2],
            vel_along_y[0],
            vel_along_y[1],
            vel_along_y[2],
            velocity[0],
            velocity[1],
            velocity[2],
        )
        stress = stress + time_step * modulus * rates
        fault_layer = jnp.where(minus_device, traction_full, stress[3][:, last_row, :])
        stress = stress.at[3, :, last_row, :].set(fault_layer)
    return (velocity, stress, rate, state_now)


def solution(mesh):
    return jax.shard_map(
        local,
        mesh=mesh,
        in_specs=(
            P(None, "strike", "normal", None),
            P(None, "strike", "normal", None),
            P("strike", "normal", None),
            P("strike", "normal", None),
            P(("strike", "normal"), None),
            P(("strike", "normal"), None),
            P(("strike", "normal"), None),
            P(),
        ),
        out_specs=(
            P(None, "strike", "normal", None),
            P(None, "strike", "normal", None),
            P(("strike", "normal"), None),
            P(("strike", "normal"), None),
        ),
        check_vma=False,
    )
```

profile of v0, /device:TPU:29, one launch (start us, length us, event | category | flops | bytes accessed | tf_op | source)
XLA Modules:
  0.0 442.2 jit_solution(4840027687795716641)
XLA Ops:
  7.2 6.1 %constant_dynamic-update-slice_fusion.1 = (f32[6,34,16,384]{3,1,2,0:T(8,128)}, f32[6,32,16,384]{3,1,2,0:T(8,128)S(1)}) fusion(f32[6,32,16,384]{3,2,1,0:T(8,128)} %param.25), kind=kLoop, calls=%fused_computation.427 | loop fusion | bytes 14155776
  13.3 2.2 copy-done.3
  16.5 3.5 collective-permute-start.1
  20.0 3.3 collective-permute-start
  23.8 4.1 collective-permute-done.1
  27.9 7.7 %collective-permute-done = f32[6,2,16,384]{3,1,2,0:T(2,128)S(1)} collective-permute-done((f32[6,2,16,384]{3,1,2,0:T(2,128)S(1)}, f32[6,2,16,384]{3,1,2,0:T(2,128)S(1)}, u32[]{:S(2)}, u32[]{:S(2)}) %collective-permute-start) | collective-permute-done | bytes 294944 | tf_op jit(solution)/shard_map/ppermute | solution.py:24
  37.6 4.0 collective-permute-start.2
  44.4 4.8 %collective-permute-done.2 = f32[6,36,2,384]{3,2,1,0:T(2,128)S(1)} collective-permute-done((f32[6,36,2,384]{3,2,1,0:T(2,128)S(1)}, f32[6,36,2,384]{3,2,1,0:T(2,128)S(1)}, u32[]{:S(2)}, u32[]{:S(2)}) %collective-permute-start.2) | collective-permute-done | bytes 663584 | tf_op jit(solution)/shard_map/ppermute | solution.py:22
  49.3 6.8 %collective-permute-done.3 = f32[6,36,2,384]{3,2,1,0:T(2,128)S(1)} collective-permute-done((f32[6,36,2,384]{3,2,1,0:T(2,128)S(1)}, f32[6,36,2,384]{3,2,1,0:T(2,128)S(1)}, u32[]{:S(2)}, u32[]{:S(2)}) %collective-permute-start.3) | collective-permute-done | bytes 663584 | tf_op jit(solution)/shard_map/ppermute | solution.py:24
  62.5 108.5 %all-reduce.15.cloned.1.call-done = f32[3,32,384]{2,1,0:T(8,128)} async-done(((f32[3,32,384]{2,1,0:T(8,128)}), f32[3,32,384]{2,1,0:T(8,128)}) %all-reduce.15.cloned.1.call-update) | async-done | bytes 147472 | tf_op jit(solution)/shard_map/psum | solution.py:144
  172.7 14.7 %all_gather.6 = f32[3,32,384]{2,0,1:T(4,128)S(1)} all-gather(f32[3,2,384]{2,0,1:T(4,128)S(1)} %copy.49), channel_id=1, replica_groups=mesh['strike'=8,'normal'=16] {'normal'}, dimensions={1}, use_global_device_ids=true | all-gather | bytes 156672 | tf_op jit(solution)/shard_map/all_gather | solution.py:149
  189.3 3.2 collective-permute-start.4
  192.5 3.6 collective-permute-start.5
  198.0 3.9 collective-permute-done.5
  202.0 6.8 %collective-permute-start.6 = (f32[3,36,2,384]{3,1,2,0:T(8,128)S(1)}, f32[3,36,2,384]{3,1,2,0:T(8,128)S(1)}, u32[]{:S(2)}, u32[]{:S(2)}) collective-permute-start(f32[3,36,2,384]{3,1,2,0:T(8,128)S(1)} %get-tuple-element.154), channel_id=1, source_target_pairs={{0,1},{1,2},{2,3},{3,4},{4,5},{5,6},{6,7},{7,8},{8,9},{9,10},{10,1... | collective-permute-start | bytes 995336 | tf_op jit(solution)/shard_map/ppermute | solution.py:22
  208.7 2.1 collective-permute-start.7
  213.2 6.5 %collective-permute-done.7 = f32[3,36,2,384]{3,1,2,0:T(8,128)S(1)} collective-permute-done((f32[3,36,2,384]{3,1,2,0:T(8,128)S(1)}, f32[3,36,2,384]{3,1,2,0:T(8,128)S(1)}, u32[]{:S(2)}, u32[]{:S(2)}) %collective-permute-start.7) | collective-permute-done | bytes 331808 | tf_op jit(solution)/shard_map/ppermute | solution.py:24
  228.3 5.8 %collective-permute-start.9 = (f32[6,2,16,384]{3,1,2,0:T(2,128)S(1)}, f32[6,2,16,384]{3,1,2,0:T(2,128)S(1)}, u32[]{:S(2)}, u32[]{:S(2)}) collective-permute-start(f32[6,2,16,384]{3,1,2,0:T(2,128)S(1)} %get-tuple-element.136), channel_id=1, source_target_pairs={{0,16},{16,32},{32,48},{48,64},{64,80},{80,96},{96,112},{1,17},{17... | collective-permute-start | bytes 884744 | tf_op jit(solution)/shard_map/ppermute | solution.py:22
  234.0 3.0 collective-permute-done.8
  238.8 4.1 collective-permute-start.10
  245.4 5.1 %collective-permute-done.10 = f32[6,36,2,384]{3,2,1,0:T(2,128)S(1)} collective-permute-done((f32[6,36,2,384]{3,2,1,0:T(2,128)S(1)}, f32[6,36,2,384]{3,2,1,0:T(2,128)S(1)}, u32[]{:S(2)}, u32[]{:S(2)}) %collective-permute-start.10) | collective-permute-done | bytes 663584 | tf_op jit(solution)/shard_map/ppermute | solution.py:22
  250.5 6.8 %collective-permute-done.11 = f32[6,36,2,384]{3,2,1,0:T(2,128)S(1)} collective-permute-done((f32[6,36,2,384]{3,2,1,0:T(2,128)S(1)}, f32[6,36,2,384]{3,2,1,0:T(2,128)S(1)}, u32[]{:S(2)}, u32[]{:S(2)}) %collective-permute-start.11) | collective-permute-done | bytes 663584 | tf_op jit(solution)/shard_map/ppermute | solution.py:24
  263.5 111.2 %all-reduce.17.cloned.1.call-done = f32[3,32,384]{2,1,0:T(8,128)} async-done(((f32[3,32,384]{2,1,0:T(8,128)}), f32[3,32,384]{2,1,0:T(8,128)}) %all-reduce.17.cloned.1.call-update) | async-done | bytes 147472 | tf_op jit(solution)/shard_map/psum | solution.py:144
  377.0 14.9 %all_gather.7 = f32[3,32,384]{2,0,1:T(4,128)S(1)} all-gather(f32[3,2,384]{2,0,1:T(4,128)S(1)} %copy.60), channel_id=1, replica_groups=mesh['strike'=8,'normal'=16] {'normal'}, dimensions={1}, use_global_device_ids=true | all-gather | bytes 156672 | tf_op jit(solution)/shard_map/all_gather | solution.py:149
  393.8 3.2 collective-permute-start.12
  397.0 3.6 collective-permute-start.13
  402.5 3.9 collective-permute-done.13
  406.5 6.8 %collective-permute-start.14 = (f32[3,36,2,384]{3,1,2,0:T(8,128)S(1)}, f32[3,36,2,384]{3,1,2,0:T(8,128)S(1)}, u32[]{:S(2)}, u32[]{:S(2)}) collective-permute-start(f32[3,36,2,384]{3,1,2,0:T(8,128)S(1)} %get-tuple-element.152), channel_id=1, source_target_pairs={{0,1},{1,2},{2,3},{3,4},{4,5},{5,6},{6,7},{7,8},{8,9},{9,10},{10,1... | collective-permute-start | bytes 995336 | tf_op jit(solution)/shard_map/ppermute | solution.py:22
  413.2 1.9 collective-permute-start.15
  415.2 2.8 copy.64
  418.0 6.2 %collective-permute-done.15 = f32[3,36,2,384]{3,1,2,0:T(8,128)S(1)} collective-permute-done((f32[3,36,2,384]{3,1,2,0:T(8,128)S(1)}, f32[3,36,2,384]{3,1,2,0:T(8,128)S(1)}, u32[]{:S(2)}, u32[]{:S(2)}) %collective-permute-start.15) | collective-permute-done | bytes 331808 | tf_op jit(solution)/shard_map/ppermute | solution.py:24
  430.5 4.9 %copy.65 = f32[6,32,16,384]{3,2,1,0:T(8,128)} copy(f32[6,32,16,384]{3,1,2,0:T(8,128)S(1)} %fusion.225) | data formatting | bytes 9437184
  (150 shorter events, 51.5 us)
Async XLA Ops:
  7.2 16.5 %copy-start = (f32[4,4]{1,0:T(4,128)S(1)}, f32[4,4]{1,0:T(4,128)}, u32[]{:S(2)}) copy-start(f32[4,4]{1,0:T(4,128)} %param.31) | copy-start | bytes 196
  7.2 16.1 %copy-start.13 = (f32[32,16,384]{2,1,0:T(8,128)S(1)}, f32[32,16,384]{2,1,0:T(8,128)}, u32[]{:S(2)}) copy-start(f32[32,16,384]{2,1,0:T(8,128)} %param.27) | copy-start | bytes 2359300
  7.2 16.5 %copy-start.18 = (s32[2,384]{1,0:T(2,128)S(1)}, s32[2,384]{1,0:T(2,128)}, u32[]{:S(2)}) copy-start(s32[2,384]{1,0:T(2,128)} %param.30) | copy-start | bytes 9220
  7.2 163.7 %all-reduce.15.cloned.1.call-start = ((), (), s32[]{:S(2)}) async-start(), calls=%async_computation | async-start | bytes 294912 | tf_op jit(solution)/shard_map/psum | solution.py:144
  16.5 11.5 %collective-permute-start.1 = (f32[6,2,16,384]{3,1,2,0:T(2,128)}, f32[6,2,16,384]{3,1,2,0:T(2,128)S(1)}, u32[]{:S(2)}, u32[]{:S(2)}) collective-permute-start(f32[6,2,16,384]{3,1,2,0:T(2,128)} %get-tuple-element.144), channel_id=1, source_target_pairs={{0,16},{16,32},{32,48},{48,64},{64,80},{80,96},{96,112},{1,17},{17... | collective-permute-start | bytes 884744 | tf_op jit(solution)/shard_map/ppermute | solution.py:22
  20.0 15.7 %collective-permute-start = (f32[6,2,16,384]{3,1,2,0:T(2,128)S(1)}, f32[6,2,16,384]{3,1,2,0:T(2,128)S(1)}, u32[]{:S(2)}, u32[]{:S(2)}) collective-permute-start(f32[6,2,16,384]{3,1,2,0:T(2,128)S(1)} %get-tuple-element.145), channel_id=1, source_target_pairs={{16,0},{32,16},{48,32},{64,48},{80,64},{96,80},{112,96},{17,1},{33... | collective-permute-start | bytes 884744 | tf_op jit(solution)/shard_map/ppermute | solution.py:24
  23.6 35.2 %copy-start.8 = (f32[32,16,384]{2,0,1:T(8,128)}, f32[32,16,384]{2,0,1:T(8,128)S(1)}, u32[]{:S(2)}) copy-start(f32[32,16,384]{2,0,1:T(8,128)S(1)} %copy.31) | copy-start | bytes 2359300
  23.7 20.2 %slice-start.2 = ((s8[4718592]{0:T(1024)(128)(4,1)}), s8[4194304]{0:T(1024)(128)(4,1)S(1)}, s32[]{:S(2)}) async-start(s8[4718592]{0:T(1024)(128)(4,1)} %bitcast.430), calls=%async_computation.4 | async-start | bytes 8388608
  23.8 20.1 %slice-start.3 = ((s8[4718592]{0:T(1024)(128)(4,1)}), s8[524288]{0:T(1024)(128)(4,1)S(1)}, s32[]{:S(2)}) async-start(s8[4718592]{0:T(1024)(128)(4,1)} %bitcast.430), calls=%async_computation.5 | async-start | bytes 1048576
  35.6 8.5 %slice-start.6 = ((s8[5898240]{0:T(1024)(128)(4,1)}), s8[4194304]{0:T(1024)(128)(4,1)S(1)}, s32[]{:S(2)}) async-start(s8[5898240]{0:T(1024)(128)(4,1)} %bitcast.436), calls=%async_computation.8 | async-start | bytes 8388608
  37.6 11.7 %collective-permute-start.2 = (f32[6,36,2,384]{3,2,1,0:T(2,128)S(1)}, f32[6,36,2,384]{3,2,1,0:T(2,128)S(1)}, u32[]{:S(2)}, u32[]{:S(2)}) collective-permute-start(f32[6,36,2,384]{3,2,1,0:T(2,128)S(1)} %copy.38), channel_id=1, source_target_pairs={{0,1},{1,2},{2,3},{3,4},{4,5},{5,6},{6,7},{7,8},{8,9},{9,10},{10,1... | collective-permute-start | bytes 1990664 | tf_op jit(solution)/shard_map/ppermute | solution.py:22
  42.0 14.1 %collective-permute-start.3 = (f32[6,36,2,384]{3,2,1,0:T(2,128)S(1)}, f32[6,36,2,384]{3,2,1,0:T(2,128)S(1)}, u32[]{:S(2)}, u32[]{:S(2)}) collective-permute-start(f32[6,36,2,384]{3,2,1,0:T(2,128)S(1)} %copy.39), channel_id=1, source_target_pairs={{1,0},{2,1},{3,2},{4,3},{5,4},{6,5},{7,6},{8,7},{9,8},{10,9},{11,1... | collective-permute-start | bytes 1990664 | tf_op jit(solution)/shard_map/ppermute | solution.py:24
  59.7 111.2 %copy-start.15 = (s32[2,384]{1,0:T(2,128)S(1)}, s32[2,384]{1,0:T(2,128)}, u32[]{:S(2)}) copy-start(s32[2,384]{1,0:T(2,128)} %param.29) | copy-start | bytes 9220
  59.7 111.2 %copy-start.17 = (f32[2,384]{1,0:T(2,128)S(1)}, f32[2,384]{1,0:T(2,128)}, u32[]{:S(2)}) copy-start(f32[2,384]{1,0:T(2,128)} %param.28) | copy-start | bytes 9220
  62.4 312.3 %all-reduce.17.cloned.1.call-start = ((), (), s32[]{:S(2)}) async-start(), calls=%async_computation.1 | async-start | bytes 294912 | tf_op jit(solution)/shard_map/psum | solution.py:144
  170.9 39.9 %copy-start.14 = (f32[32,16,384]{2,1,0:T(8,128)S(1)}, f32[32,16,384]{2,1,0:T(8,128)}, u32[]{:S(2)}) copy-start(f32[32,16,384]{2,1,0:T(8,128)} %param.26) | copy-start | bytes 2359300
  189.2 32.7 %copy-start.4 = (f32[3,32,16,384]{3,1,2,0:T(8,128)}, f32[3,32,16,384]{3,1,2,0:T(8,128)S(1)}, u32[]{:S(2)}) copy-start(f32[3,32,16,384]{3,1,2,0:T(8,128)S(1)} %constant_dynamic-update-slice_fusion.3) | copy-start | bytes 7077892
  189.3 8.7 %collective-permute-start.4 = (f32[3,2,16,384]{3,1,2,0:T(2,128)S(1)}, f32[3,2,16,384]{3,1,2,0:T(2,128)S(1)}, u32[]{:S(2)}, u32[]{:S(2)}) collective-permute-start(f32[3,2,16,384]{3,1,2,0:T(2,128)S(1)} %get-tuple-element.162), channel_id=1, source_target_pairs={{0,16},{16,32},{32,48},{48,64},{64,80},{80,96},{96,112},{1,17},{17... | collective-permute-start | bytes 442376 | tf_op jit(solution)/shard_map/ppermute | solution.py:22
  192.5 9.4 %collective-permute-start.5 = (f32[3,2,16,384]{3,1,2,0:T(2,128)S(1)}, f32[3,2,16,384]{3,1,2,0:T(2,128)S(1)}, u32[]{:S(2)}, u32[]{:S(2)}) collective-permute-start(f32[3,2,16,384]{3,1,2,0:T(2,128)S(1)} %get-tuple-element.163), channel_id=1, source_target_pairs={{16,0},{32,16},{48,32},{64,48},{80,64},{96,80},{112,96},{17,1},{33... | collective-permute-start | bytes 442376 | tf_op jit(solution)/shard_map/ppermute | solution.py:24
  202.0 11.2 %collective-permute-start.6 = (f32[3,36,2,384]{3,1,2,0:T(8,128)S(1)}, f32[3,36,2,384]{3,1,2,0:T(8,128)S(1)}, u32[]{:S(2)}, u32[]{:S(2)}) collective-permute-start(f32[3,36,2,384]{3,1,2,0:T(8,128)S(1)} %get-tuple-element.154), channel_id=1, source_target_pairs={{0,1},{1,2},{2,3},{3,4},{4,5},{5,6},{6,7},{7,8},{8,9},{9,10},{10,1... | collective-permute-start | bytes 995336 | tf_op jit(solution)/shard_map/ppermute | solution.py:22
  208.7 10.9 %collective-permute-start.7 = (f32[3,36,2,384]{3,1,2,0:T(8,128)S(1)}, f32[3,36,2,384]{3,1,2,0:T(8,128)S(1)}, u32[]{:S(2)}, u32[]{:S(2)}) collective-permute-start(f32[3,36,2,384]{3,1,2,0:T(8,128)S(1)} %get-tuple-element.155), channel_id=1, source_target_pairs={{1,0},{2,1},{3,2},{4,3},{5,4},{6,5},{7,6},{8,7},{9,8},{10,9},{11,1... | collective-permute-start | bytes 995336 | tf_op jit(solution)/shard_map/ppermute | solution.py:24
  211.2 12.1 %copy-start.6 = (f32[32,16,384]{2,0,1:T(8,128)}, f32[32,16,384]{2,0,1:T(8,128)S(1)}, u32[]{:S(2)}) copy-start(f32[32,16,384]{2,0,1:T(8,128)S(1)} %copy.52) | copy-start | bytes 2359300
  226.1 33.3 %copy-start.2 = (f32[6,32,16,384]{3,1,2,0:T(8,128)}, f32[6,32,16,384]{3,1,2,0:T(8,128)S(1)}, u32[]{:S(2)}) copy-start(f32[6,32,16,384]{3,1,2,0:T(8,128)S(1)} %fusion.228) | copy-start | bytes 14155780
  226.3 10.7 %collective-permute-start.8 = (f32[6,2,16,384]{3,1,2,0:T(2,128)S(1)}, f32[6,2,16,384]{3,1,2,0:T(2,128)S(1)}, u32[]{:S(2)}, u32[]{:S(2)}) collective-permute-start(f32[6,2,16,384]{3,1,2,0:T(2,128)S(1)} %get-tuple-element.137), channel_id=1, source_target_pairs={{16,0},{32,16},{48,32},{64,48},{80,64},{96,80},{112,96},{17,1},{33... | collective-permute-start | bytes 884744 | tf_op jit(solution)/shard_map/ppermute | solution.py:24
  228.3 10.0 %collective-permute-start.9 = (f32[6,2,16,384]{3,1,2,0:T(2,128)S(1)}, f32[6,2,16,384]{3,1,2,0:T(2,128)S(1)}, u32[]{:S(2)}, u32[]{:S(2)}) collective-permute-start(f32[6,2,16,384]{3,1,2,0:T(2,128)S(1)} %get-tuple-element.136), channel_id=1, source_target_pairs={{0,16},{16,32},{32,48},{48,64},{64,80},{80,96},{96,112},{1,17},{17... | collective-permute-start | bytes 884744 | tf_op jit(solution)/shard_map/ppermute | solution.py:22
  238.8 11.7 %collective-permute-start.10 = (f32[6,36,2,384]{3,2,1,0:T(2,128)S(1)}, f32[6,36,2,384]{3,2,1,0:T(2,128)S(1)}, u32[]{:S(2)}, u32[]{:S(2)}) collective-permute-start(f32[6,36,2,384]{3,2,1,0:T(2,128)S(1)} %copy.55), channel_id=1, source_target_pairs={{0,1},{1,2},{2,3},{3,4},{4,5},{5,6},{6,7},{7,8},{8,9},{9,10},{10,1... | collective-permute-start | bytes 1990664 | tf_op jit(solution)/shard_map/ppermute | solution.py:22
  243.2 14.1 %collective-permute-start.11 = (f32[6,36,2,384]{3,2,1,0:T(2,128)S(1)}, f32[6,36,2,384]{3,2,1,0:T(2,128)S(1)}, u32[]{:S(2)}, u32[]{:S(2)}) collective-permute-start(f32[6,36,2,384]{3,2,1,0:T(2,128)S(1)} %copy.56), channel_id=1, source_target_pairs={{1,0},{2,1},{3,2},{4,3},{5,4},{6,5},{7,6},{8,7},{9,8},{10,9},{11,1... | collective-permute-start | bytes 1990664 | tf_op jit(solution)/shard_map/ppermute | solution.py:24
  376.2 41.7 %copy-start.16 = (f32[2,384]{1,0:T(2,128)}, f32[2,384]{1,0:T(2,128)S(1)}, u32[]{:S(2)}) copy-start(f32[2,384]{1,0:T(2,128)S(1)} %get-tuple-element.109) | copy-start | bytes 9220
  393.8 8.7 %collective-permute-start.12 = (f32[3,2,16,384]{3,1,2,0:T(2,128)S(1)}, f32[3,2,16,384]{3,1,2,0:T(2,128)S(1)}, u32[]{:S(2)}, u32[]{:S(2)}) collective-permute-start(f32[3,2,16,384]{3,1,2,0:T(2,128)S(1)} %get-tuple-element.157), channel_id=1, source_target_pairs={{0,16},{16,32},{32,48},{48,64},{64,80},{80,96},{96,112},{1,17},{17... | collective-permute-start | bytes 442376 | tf_op jit(solution)/shard_map/ppermute | solution.py:22
  397.0 9.4 %collective-permute-start.13 = (f32[3,2,16,384]{3,1,2,0:T(2,128)S(1)}, f32[3,2,16,384]{3,1,2,0:T(2,128)S(1)}, u32[]{:S(2)}, u32[]{:S(2)}) collective-permute-start(f32[3,2,16,384]{3,1,2,0:T(2,128)S(1)} %get-tuple-element.158), channel_id=1, source_target_pairs={{16,0},{32,16},{48,32},{64,48},{80,64},{96,80},{112,96},{17,1},{33... | collective-permute-start | bytes 442376 | tf_op jit(solution)/shard_map/ppermute | solution.py:24
  406.5 11.5 %collective-permute-start.14 = (f32[3,36,2,384]{3,1,2,0:T(8,128)S(1)}, f32[3,36,2,384]{3,1,2,0:T(8,128)S(1)}, u32[]{:S(2)}, u32[]{:S(2)}) collective-permute-start(f32[3,36,2,384]{3,1,2,0:T(8,128)S(1)} %get-tuple-element.152), channel_id=1, source_target_pairs={{0,1},{1,2},{2,3},{3,4},{4,5},{5,6},{6,7},{7,8},{8,9},{9,10},{10,1... | collective-permute-start | bytes 995336 | tf_op jit(solution)/shard_map/ppermute | solution.py:22
  413.2 10.9 %collective-permute-start.15 = (f32[3,36,2,384]{3,1,2,0:T(8,128)S(1)}, f32[3,36,2,384]{3,1,2,0:T(8,128)S(1)}, u32[]{:S(2)}, u32[]{:S(2)}) collective-permute-start(f32[3,36,2,384]{3,1,2,0:T(8,128)S(1)} %get-tuple-element.153), channel_id=1, source_target_pairs={{1,0},{2,1},{3,2},{4,3},{5,4},{6,5},{7,6},{8,7},{9,8},{10,9},{11,1... | collective-permute-start | bytes 995336 | tf_op jit(solution)/shard_map/ppermute | solution.py:24
  (13 other events, 32.5 us)
Sparse Core Ops, SparseCore 0:
  62.5 108.3 all-reduce.14
  263.6 111.0 all-reduce.16
where the time goes:
time: 443 us; the launch traced here: 442 us
  waiting for transfers between devices  285 us (64%)
  starting transfers between devices  57.7 us (13%)
  blocking collectives  29.6 us (7%)
  other arithmetic  27.8 us (6%)
  local copies, waits for them, and re-layouts  26.7 us (6%)
  between operations  14.9 us (3%)
    psum x2, waiting for transfers between devices, local(): rows_all = lax.psum(contrib, 'normal')  220 us
    ppermute x8, waiting for transfers between devices, with_halo(): lax.ppermute(head, axis, [((i + 1) % count, i) for i in range(ends)])  44.8 us
    ppermute x8, starting transfers between devices, with_halo(): lax.ppermute(tail, axis, [(i, (i + 1) % count) for i in range(ends)])  37.2 us
    all_gather x2, blocking collectives, local(): lax.all_gather(jnp.stack((minus_own, plus_own, traction_own)), 'normal',...  29.6 us
    unnamed x57, local copies, waits for them, and re-layouts  21.8 us
    ppermute x8, waiting for transfers between devices, with_halo(): lax.ppermute(tail, axis, [(i, (i + 1) % count) for i in range(ends)])  20.9 us
    ppermute x8, starting transfers between devices, with_halo(): lax.ppermute(head, axis, [((i + 1) % count, i) for i in range(ends)])  20.3 us
  transfers between devices with their start and end apart: 18, of which 17 were waited for; matrix products, arithmetic and copies ran while one was open for 1% of the time, Pallas kernels for 0%

commit v1 on v0

--- a/solution.py
+++ b/solution.py
@@ -141,7 +141,7 @@
                 jnp.where(minus_device, traction_row, blank),
             )
         )
-        rows_all = lax.psum(contrib, "normal")
+        rows_all = jnp.sum(lax.all_gather(contrib, "normal"), axis=0)
         mine = lax.dynamic_slice_in_dim(rows_all, position * owned_rows, owned_rows, 1)
         rate, traction_own, minus_own, plus_own, state_now = friction(
             mine[0], mine[1], mine[2], state_now, mask_now, params

time: 443 us -> 310 us (0.70)
  waiting for transfers between devices: 285 us -> 132 us
  local copies, waits for them, and re-layouts: 26.7 us -> 37 us
    psum x2 -> x0, waiting for transfers between devices: 220 us -> none  [local(): rows_all = lax.psum(contrib, 'normal')]
    all_gather x0 -> x2, waiting for transfers between devices: none -> 71.4 us  [local(): rows_all = jnp.sum(lax.all_gather(contrib, 'normal'), axis=0)]
    scatter x0 -> x6, local copies, waits for them, and re-layouts: none -> 12 us  [the longest x4 7.71 us: local(): vel_x = vel_x.at[:, last_row, :].set(new_last).at[:, 0, :].set(new_first)]
    ppermute x8, waiting for transfers between devices: 44.8 us -> 39.1 us  [with_halo(): lax.ppermute(head, axis, [((i + 1) % count, i) for i in range(ends)])]
    unnamed x57 -> x64, local copies, waits for them, and re-layouts: 21.8 us -> 16.9 us
  transfers between devices with their start and end apart: 18 -> 18, of which waited for: 17 -> 18; matrix products, arithmetic and copies ran while one was open for 1% -> 3% of each run, Pallas kernels for 0% -> 0%
where the time goes in v1:
time: 310 us; the launch traced here: 309 us
  waiting for transfers between devices  132 us (43%)
  starting transfers between devices  59.5 us (19%)
  local copies, waits for them, and re-layouts  37 us (12%)
  blocking collectives  33 us (11%)
  other arithmetic  31.6 us (10%)
  between operations  14.9 us (5%)
    all_gather x2, waiting for transfers between devices, local(): rows_all = jnp.sum(lax.all_gather(contrib, 'normal'), axis=0)  71.4 us
    ppermute x8, starting transfers between devices, with_halo(): lax.ppermute(tail, axis, [(i, (i + 1) % count) for i in range(ends)])  39.8 us
    ppermute x8, waiting for transfers between devices, with_halo(): lax.ppermute(head, axis, [((i + 1) % count, i) for i in range(ends)])  39.1 us
    all_gather x2, blocking collectives, local(): lax.all_gather(jnp.stack((minus_own, plus_own, traction_own)), 'normal',...  33 us
    ppermute x8, waiting for transfers between devices, with_halo(): lax.ppermute(tail, axis, [(i, (i + 1) % count) for i in range(ends)])  22 us
    ppermute x8, starting transfers between devices, with_halo(): lax.ppermute(head, axis, [((i + 1) % count, i) for i in range(ends)])  19.6 us
    unnamed x64, local copies, waits for them, and re-layouts  16.9 us
    another operation x6, other arithmetic, accelerate(): return jnp.stack((accel_x, accel_y, accel_z))  8.25 us
  transfers between devices with their start and end apart: 18, of which 18 were waited for; matrix products, arithmetic and copies ran while one was open for 3% of the time, Pallas kernels for 0%

profile of v1, /device:TPU:29, one launch (start us, length us, event | category | flops | bytes accessed | tf_op | source)
XLA Modules:
  0.0 308.7 jit_solution(17931072263525374201)
XLA Ops:
  8.3 3.5 %collective-permute-start.1 = (f32[6,2,16,384]{3,2,1,0:T(8,128)S(1)}, f32[6,2,16,384]{3,2,1,0:T(8,128)S(1)}, u32[]{:S(2)}, u32[]{:S(2)}) collective-permute-start(f32[6,2,16,384]{3,2,1,0:T(8,128)S(1)} %get-tuple-element.142), channel_id=1, source_target_pairs={{0,16},{16,32},{32,48},{48,64},{64,80},{80,96},{96,112},{1,17},{17... | collective-permute-start | bytes 884744 | tf_op jit(solution)/shard_map/ppermute | solution.py:22
  11.8 3.3 %collective-permute-start = (f32[6,2,16,384]{3,2,1,0:T(8,128)S(1)}, f32[6,2,16,384]{3,2,1,0:T(8,128)S(1)}, u32[]{:S(2)}, u32[]{:S(2)}) collective-permute-start(f32[6,2,16,384]{3,2,1,0:T(8,128)S(1)} %get-tuple-element.141), channel_id=1, source_target_pairs={{16,0},{32,16},{48,32},{64,48},{80,64},{96,80},{112,96},{17,1},{33... | collective-permute-start | bytes 884744 | tf_op jit(solution)/shard_map/ppermute | solution.py:24
  15.1 4.5 %collective-permute-done.1 = f32[6,2,16,384]{3,2,1,0:T(8,128)S(1)} collective-permute-done((f32[6,2,16,384]{3,2,1,0:T(8,128)S(1)}, f32[6,2,16,384]{3,2,1,0:T(8,128)S(1)}, u32[]{:S(2)}, u32[]{:S(2)}) %collective-permute-start.1) | collective-permute-done | bytes 294944 | tf_op jit(solution)/shard_map/ppermute | solution.py:22
  19.7 5.1 %constant_dynamic-update-slice_fusion.1 = (f32[6,34,16,384]{3,2,1,0:T(8,128)}, f32[6,36,16,384]{3,2,1,0:T(8,128)S(1)}, f32[6,34,16,384]{3,2,1,0:T(8,128)S(1)}) fusion(f32[6,32,16,384]{3,2,1,0:T(8,128)} %param.25, f32[6,36,16,384]{3,2,1,0:T(8,128)S(1)} %get-tuple-element.170, f32[6,34,16,384]{3,2,1,0:T(8,128)S(1)} %get-tuple-element.169), kind=kLoop, calls=%fused_computation.419 | loop fusion | bytes 18874368
  24.8 2.5 collective-permute-done
  28.0 2.4 copy-done.7
  30.9 3.9 %collective-permute-start.2 = (f32[6,36,2,384]{3,2,1,0:T(2,128)S(1)}, f32[6,36,2,384]{3,2,1,0:T(2,128)S(1)}, u32[]{:S(2)}, u32[]{:S(2)}) collective-permute-start(f32[6,36,2,384]{3,2,1,0:T(2,128)S(1)} %get-tuple-element.126), channel_id=1, source_target_pairs={{0,1},{1,2},{2,3},{3,4},{4,5},{5,6},{6,7},{7,8},{8,9},{9,10},{10,1... | collective-permute-start | bytes 1990664 | tf_op jit(solution)/shard_map/ppermute | solution.py:22
  36.8 2.5 slice_bitcast_fusion.14
  39.3 3.0 collective-permute-done.2
  42.4 6.5 %collective-permute-done.3 = f32[6,36,2,384]{3,2,1,0:T(2,128)S(1)} collective-permute-done((f32[6,36,2,384]{3,2,1,0:T(2,128)S(1)}, f32[6,36,2,384]{3,2,1,0:T(2,128)S(1)}, u32[]{:S(2)}, u32[]{:S(2)}) %collective-permute-start.3) | collective-permute-done | bytes 663584 | tf_op jit(solution)/shard_map/ppermute | solution.py:24
  49.5 2.2 fusion.10
  58.2 34.8 %all-gather.5.cloned.1.call-done = f32[48,32,384]{2,1,0:T(8,128)} async-done(((f32[3,32,384]{2,1,0:T(8,128)}), f32[48,32,384]{2,1,0:T(8,128)}) %all-gather.5.cloned.1.call-update) | async-done | bytes 2359312 | tf_op jit(solution)/shard_map/all_gather | solution.py:144
  95.0 16.5 %all_gather.20 = f32[3,32,384]{2,0,1:T(4,128)S(1)} all-gather(f32[3,2,384]{2,0,1:T(4,128)S(1)} %copy.34), channel_id=1, replica_groups=mesh['strike'=8,'normal'=16] {'normal'}, dimensions={1}, use_global_device_ids=true | all-gather | bytes 156672 | tf_op jit(solution)/shard_map/all_gather | solution.py:149
  117.7 3.8 %collective-permute-start.4 = (f32[3,2,16,384]{3,2,1,0:T(8,128)S(1)}, f32[3,2,16,384]{3,2,1,0:T(8,128)S(1)}, u32[]{:S(2)}, u32[]{:S(2)}) collective-permute-start(f32[3,2,16,384]{3,2,1,0:T(8,128)S(1)} %get-tuple-element.159), channel_id=1, source_target_pairs={{0,16},{16,32},{32,48},{48,64},{64,80},{80,96},{96,112},{1,17},{17... | collective-permute-start | bytes 442376 | tf_op jit(solution)/shard_map/ppermute | solution.py:22
  121.4 3.2 %collective-permute-start.5 = (f32[3,2,16,384]{3,2,1,0:T(8,128)S(1)}, f32[3,2,16,384]{3,2,1,0:T(8,128)S(1)}, u32[]{:S(2)}, u32[]{:S(2)}) collective-permute-start(f32[3,2,16,384]{3,2,1,0:T(8,128)S(1)} %get-tuple-element.160), channel_id=1, source_target_pairs={{16,0},{32,16},{48,32},{64,48},{80,64},{96,80},{112,96},{17,1},{33... | collective-permute-start | bytes 442376 | tf_op jit(solution)/shard_map/ppermute | solution.py:24
  126.5 4.2 %collective-permute-done.5 = f32[3,2,16,384]{3,2,1,0:T(8,128)S(1)} collective-permute-done((f32[3,2,16,384]{3,2,1,0:T(8,128)S(1)}, f32[3,2,16,384]{3,2,1,0:T(8,128)S(1)}, u32[]{:S(2)}, u32[]{:S(2)}) %collective-permute-start.5) | collective-permute-done | bytes 147488 | tf_op jit(solution)/shard_map/ppermute | solution.py:24
  130.9 7.5 %collective-permute-start.6 = (f32[3,36,2,384]{3,2,1,0:T(2,128)S(1)}, f32[3,36,2,384]{3,2,1,0:T(2,128)S(1)}, u32[]{:S(2)}, u32[]{:S(2)}) collective-permute-start(f32[3,36,2,384]{3,2,1,0:T(2,128)S(1)} %get-tuple-element.151), channel_id=1, source_target_pairs={{0,1},{1,2},{2,3},{3,4},{4,5},{5,6},{6,7},{7,8},{8,9},{9,10},{10,1... | collective-permute-start | bytes 995336 | tf_op jit(solution)/shard_map/ppermute | solution.py:22
  142.4 6.5 %collective-permute-done.7 = f32[3,36,2,384]{3,2,1,0:T(2,128)S(1)} collective-permute-done((f32[3,36,2,384]{3,2,1,0:T(2,128)S(1)}, f32[3,36,2,384]{3,2,1,0:T(2,128)S(1)}, u32[]{:S(2)}, u32[]{:S(2)}) %collective-permute-start.7) | collective-permute-done | bytes 331808 | tf_op jit(solution)/shard_map/ppermute | solution.py:24
  153.8 2.2 copy-done.2
  161.3 6.0 %collective-permute-start.9 = (f32[6,2,16,384]{3,2,1,0:T(8,128)S(1)}, f32[6,2,16,384]{3,2,1,0:T(8,128)S(1)}, u32[]{:S(2)}, u32[]{:S(2)}) collective-permute-start(f32[6,2,16,384]{3,2,1,0:T(8,128)S(1)} %get-tuple-element.132), channel_id=1, source_target_pairs={{0,16},{16,32},{32,48},{48,64},{64,80},{80,96},{96,112},{1,17},{17... | collective-permute-start | bytes 884744 | tf_op jit(solution)/shard_map/ppermute | solution.py:22
  171.2 2.9 pad_maximum_fusion.22
  174.1 4.1 %collective-permute-start.10 = (f32[6,36,2,384]{3,2,1,0:T(2,128)S(1)}, f32[6,36,2,384]{3,2,1,0:T(2,128)S(1)}, u32[]{:S(2)}, u32[]{:S(2)}) collective-permute-start(f32[6,36,2,384]{3,2,1,0:T(2,128)S(1)} %get-tuple-element.124), channel_id=1, source_target_pairs={{0,1},{1,2},{2,3},{3,4},{4,5},{5,6},{6,7},{7,8},{8,9},{9,10},{10,1... | collective-permute-start | bytes 1990664 | tf_op jit(solution)/shard_map/ppermute | solution.py:22
  180.5 5.3 %collective-permute-done.10 = f32[6,36,2,384]{3,2,1,0:T(2,128)S(1)} collective-permute-done((f32[6,36,2,384]{3,2,1,0:T(2,128)S(1)}, f32[6,36,2,384]{3,2,1,0:T(2,128)S(1)}, u32[]{:S(2)}, u32[]{:S(2)}) %collective-permute-start.10) | collective-permute-done | bytes 663584 | tf_op jit(solution)/shard_map/ppermute | solution.py:22
  185.8 6.5 %collective-permute-done.11 = f32[6,36,2,384]{3,2,1,0:T(2,128)S(1)} collective-permute-done((f32[6,36,2,384]{3,2,1,0:T(2,128)S(1)}, f32[6,36,2,384]{3,2,1,0:T(2,128)S(1)}, u32[]{:S(2)}, u32[]{:S(2)}) %collective-permute-start.11) | collective-permute-done | bytes 663584 | tf_op jit(solution)/shard_map/ppermute | solution.py:24
  199.1 36.7 %all-gather.7.cloned.1.call-done = f32[48,32,384]{2,1,0:T(8,128)} async-done(((f32[3,32,384]{2,1,0:T(8,128)}), f32[48,32,384]{2,1,0:T(8,128)}) %all-gather.7.cloned.1.call-update) | async-done | bytes 2359312 | tf_op jit(solution)/shard_map/all_gather | solution.py:144
  238.4 16.5 %all_gather.23 = f32[3,32,384]{2,0,1:T(4,128)S(1)} all-gather(f32[3,2,384]{2,0,1:T(4,128)S(1)} %copy.37), channel_id=1, replica_groups=mesh['strike'=8,'normal'=16] {'normal'}, dimensions={1}, use_global_device_ids=true | all-gather | bytes 156672 | tf_op jit(solution)/shard_map/all_gather | solution.py:149
  261.0 3.6 %collective-permute-start.12 = (f32[3,2,16,384]{3,2,1,0:T(8,128)S(1)}, f32[3,2,16,384]{3,2,1,0:T(8,128)S(1)}, u32[]{:S(2)}, u32[]{:S(2)}) collective-permute-start(f32[3,2,16,384]{3,2,1,0:T(8,128)S(1)} %get-tuple-element.154), channel_id=1, source_target_pairs={{0,16},{16,32},{32,48},{48,64},{64,80},{80,96},{96,112},{1,17},{17... | collective-permute-start | bytes 442376 | tf_op jit(solution)/shard_map/ppermute | solution.py:22
  264.6 3.2 %collective-permute-start.13 = (f32[3,2,16,384]{3,2,1,0:T(8,128)S(1)}, f32[3,2,16,384]{3,2,1,0:T(8,128)S(1)}, u32[]{:S(2)}, u32[]{:S(2)}) collective-permute-start(f32[3,2,16,384]{3,2,1,0:T(8,128)S(1)} %get-tuple-element.155), channel_id=1, source_target_pairs={{16,0},{32,16},{48,32},{64,48},{80,64},{96,80},{112,96},{17,1},{33... | collective-permute-start | bytes 442376 | tf_op jit(solution)/shard_map/ppermute | solution.py:24
  269.7 4.2 %collective-permute-done.13 = f32[3,2,16,384]{3,2,1,0:T(8,128)S(1)} collective-permute-done((f32[3,2,16,384]{3,2,1,0:T(8,128)S(1)}, f32[3,2,16,384]{3,2,1,0:T(8,128)S(1)}, u32[]{:S(2)}, u32[]{:S(2)}) %collective-permute-start.13) | collective-permute-done | bytes 147488 | tf_op jit(solution)/shard_map/ppermute | solution.py:24
  274.1 7.5 %collective-permute-start.14 = (f32[3,36,2,384]{3,2,1,0:T(2,128)S(1)}, f32[3,36,2,384]{3,2,1,0:T(2,128)S(1)}, u32[]{:S(2)}, u32[]{:S(2)}) collective-permute-start(f32[3,36,2,384]{3,2,1,0:T(2,128)S(1)} %get-tuple-element.149), channel_id=1, source_target_pairs={{0,1},{1,2},{2,3},{3,4},{4,5},{5,6},{6,7},{7,8},{8,9},{9,10},{10,1... | collective-permute-start | bytes 995336 | tf_op jit(solution)/shard_map/ppermute | solution.py:22
  285.6 6.5 %collective-permute-done.15 = f32[3,36,2,384]{3,2,1,0:T(2,128)S(1)} collective-permute-done((f32[3,36,2,384]{3,2,1,0:T(2,128)S(1)}, f32[3,36,2,384]{3,2,1,0:T(2,128)S(1)}, u32[]{:S(2)}, u32[]{:S(2)}) %collective-permute-start.15) | collective-permute-done | bytes 331808 | tf_op jit(solution)/shard_map/ppermute | solution.py:24
  297.3 2.2 copy-done.13
  (154 shorter events, 70.8 us)
Async XLA Ops:
  7.2 50.9 %copy-start = (f32[4,4]{1,0:T(4,128)S(1)}, f32[4,4]{1,0:T(4,128)}, u32[]{:S(2)}) copy-start(f32[4,4]{1,0:T(4,128)} %param.31) | copy-start | bytes 196
  7.2 85.8 %all-gather.5.cloned.1.call-start = ((), (), s32[]{:S(2)}) async-start(), calls=%async_computation | async-start | bytes 2506752 | tf_op jit(solution)/shard_map/all_gather | solution.py:144
  8.3 11.3 %collective-permute-start.1 = (f32[6,2,16,384]{3,2,1,0:T(8,128)S(1)}, f32[6,2,16,384]{3,2,1,0:T(8,128)S(1)}, u32[]{:S(2)}, u32[]{:S(2)}) collective-permute-start(f32[6,2,16,384]{3,2,1,0:T(8,128)S(1)} %get-tuple-element.142), channel_id=1, source_target_pairs={{0,16},{16,32},{32,48},{48,64},{64,80},{80,96},{96,112},{1,17},{17... | collective-permute-start | bytes 884744 | tf_op jit(solution)/shard_map/ppermute | solution.py:22
  11.8 15.5 %collective-permute-start = (f32[6,2,16,384]{3,2,1,0:T(8,128)S(1)}, f32[6,2,16,384]{3,2,1,0:T(8,128)S(1)}, u32[]{:S(2)}, u32[]{:S(2)}) collective-permute-start(f32[6,2,16,384]{3,2,1,0:T(8,128)S(1)} %get-tuple-element.141), channel_id=1, source_target_pairs={{16,0},{32,16},{48,32},{64,48},{80,64},{96,80},{112,96},{17,1},{33... | collective-permute-start | bytes 884744 | tf_op jit(solution)/shard_map/ppermute | solution.py:24
  24.8 11.9 %copy-start.19 = (f32[32,16,384]{2,1,0:T(8,128)S(1)}, f32[32,16,384]{2,1,0:T(8,128)}, u32[]{:S(2)}) copy-start(f32[32,16,384]{2,1,0:T(8,128)} %param.27) | copy-start | bytes 2359300
  30.9 11.5 %collective-permute-start.2 = (f32[6,36,2,384]{3,2,1,0:T(2,128)S(1)}, f32[6,36,2,384]{3,2,1,0:T(2,128)S(1)}, u32[]{:S(2)}, u32[]{:S(2)}) collective-permute-start(f32[6,36,2,384]{3,2,1,0:T(2,128)S(1)} %get-tuple-element.126), channel_id=1, source_target_pairs={{0,1},{1,2},{2,3},{3,4},{4,5},{5,6},{6,7},{7,8},{8,9},{9,10},{10,1... | collective-permute-start | bytes 1990664 | tf_op jit(solution)/shard_map/ppermute | solution.py:22
  34.8 14.1 %collective-permute-start.3 = (f32[6,36,2,384]{3,2,1,0:T(2,128)S(1)}, f32[6,36,2,384]{3,2,1,0:T(2,128)S(1)}, u32[]{:S(2)}, u32[]{:S(2)}) collective-permute-start(f32[6,36,2,384]{3,2,1,0:T(2,128)S(1)} %get-tuple-element.127), channel_id=1, source_target_pairs={{1,0},{2,1},{3,2},{4,3},{5,4},{6,5},{7,6},{8,7},{9,8},{10,9},{11,1... | collective-permute-start | bytes 1990664 | tf_op jit(solution)/shard_map/ppermute | solution.py:24
  36.7 12.2 %copy-start.8 = (f32[6,36,16,384]{3,2,1,0:T(8,128)S(1)}, f32[6,36,16,384]{3,2,1,0:T(8,128)}, u32[]{:S(2)}) copy-start(f32[6,36,16,384]{3,2,1,0:T(8,128)} %copy-done.7) | copy-start | bytes 15925252
  36.8 18.8 %copy-start.11 = (f32[32,16,384]{2,1,0:T(8,128)}, f32[32,16,384]{2,1,0:T(8,128)S(1)}, u32[]{:S(2)}) copy-start(f32[32,16,384]{2,1,0:T(8,128)S(1)} %broadcast_multiply_fusion.1) | copy-start | bytes 2359300
  36.8 12.6 %slice-start.2 = ((s8[4718592]{0:T(1024)(128)(4,1)}), s8[4194304]{0:T(1024)(128)(4,1)S(1)}, s32[]{:S(2)}) async-start(s8[4718592]{0:T(1024)(128)(4,1)} %bitcast.412), calls=%async_computation.4 | async-start | bytes 8388608
  39.3 10.2 %slice-start.3 = ((s8[4718592]{0:T(1024)(128)(4,1)}), s8[524288]{0:T(1024)(128)(4,1)S(1)}, s32[]{:S(2)}) async-start(s8[4718592]{0:T(1024)(128)(4,1)} %bitcast.412), calls=%async_computation.5 | async-start | bytes 1048576
  56.1 38.7 %copy-start.21 = (s32[2,384]{1,0:T(2,128)S(1)}, s32[2,384]{1,0:T(2,128)}, u32[]{:S(2)}) copy-start(s32[2,384]{1,0:T(2,128)} %param.29) | copy-start | bytes 9220
  56.1 38.7 %copy-start.23 = (f32[2,384]{1,0:T(2,128)S(1)}, f32[2,384]{1,0:T(2,128)}, u32[]{:S(2)}) copy-start(f32[2,384]{1,0:T(2,128)} %param.28) | copy-start | bytes 9220
  58.0 177.8 %all-gather.7.cloned.1.call-start = ((), (), s32[]{:S(2)}) async-start(), calls=%async_computation.1 | async-start | bytes 2506752 | tf_op jit(solution)/shard_map/all_gather | solution.py:144
  117.5 22.9 %copy-start.20 = (f32[32,16,384]{2,1,0:T(8,128)S(1)}, f32[32,16,384]{2,1,0:T(8,128)}, u32[]{:S(2)}) copy-start(f32[32,16,384]{2,1,0:T(8,128)} %param.26) | copy-start | bytes 2359300
  117.7 8.8 %collective-permute-start.4 = (f32[3,2,16,384]{3,2,1,0:T(8,128)S(1)}, f32[3,2,16,384]{3,2,1,0:T(8,128)S(1)}, u32[]{:S(2)}, u32[]{:S(2)}) collective-permute-start(f32[3,2,16,384]{3,2,1,0:T(8,128)S(1)} %get-tuple-element.159), channel_id=1, source_target_pairs={{0,16},{16,32},{32,48},{48,64},{64,80},{80,96},{96,112},{1,17},{17... | collective-permute-start | bytes 442376 | tf_op jit(solution)/shard_map/ppermute | solution.py:22
  121.4 9.3 %collective-permute-start.5 = (f32[3,2,16,384]{3,2,1,0:T(8,128)S(1)}, f32[3,2,16,384]{3,2,1,0:T(8,128)S(1)}, u32[]{:S(2)}, u32[]{:S(2)}) collective-permute-start(f32[3,2,16,384]{3,2,1,0:T(8,128)S(1)} %get-tuple-element.160), channel_id=1, source_target_pairs={{16,0},{32,16},{48,32},{64,48},{80,64},{96,80},{112,96},{17,1},{33... | collective-permute-start | bytes 442376 | tf_op jit(solution)/shard_map/ppermute | solution.py:24
  130.9 11.5 %collective-permute-start.6 = (f32[3,36,2,384]{3,2,1,0:T(2,128)S(1)}, f32[3,36,2,384]{3,2,1,0:T(2,128)S(1)}, u32[]{:S(2)}, u32[]{:S(2)}) collective-permute-start(f32[3,36,2,384]{3,2,1,0:T(2,128)S(1)} %get-tuple-element.151), channel_id=1, source_target_pairs={{0,1},{1,2},{2,3},{3,4},{4,5},{5,6},{6,7},{7,8},{8,9},{9,10},{10,1... | collective-permute-start | bytes 995336 | tf_op jit(solution)/shard_map/ppermute | solution.py:22
  138.4 10.5 %collective-permute-start.7 = (f32[3,36,2,384]{3,2,1,0:T(2,128)S(1)}, f32[3,36,2,384]{3,2,1,0:T(2,128)S(1)}, u32[]{:S(2)}, u32[]{:S(2)}) collective-permute-start(f32[3,36,2,384]{3,2,1,0:T(2,128)S(1)} %get-tuple-element.152), channel_id=1, source_target_pairs={{1,0},{2,1},{3,2},{4,3},{5,4},{6,5},{7,6},{8,7},{9,8},{10,9},{11,1... | collective-permute-start | bytes 995336 | tf_op jit(solution)/shard_map/ppermute | solution.py:24
  140.6 11.9 %copy-start.9 = (f32[32,16,384]{2,1,0:T(8,128)}, f32[32,16,384]{2,1,0:T(8,128)S(1)}, u32[]{:S(2)}) copy-start(f32[32,16,384]{2,1,0:T(8,128)S(1)} %broadcast_multiply_fusion) | copy-start | bytes 2359300
  159.3 10.1 %collective-permute-start.8 = (f32[6,2,16,384]{3,2,1,0:T(8,128)S(1)}, f32[6,2,16,384]{3,2,1,0:T(8,128)S(1)}, u32[]{:S(2)}, u32[]{:S(2)}) collective-permute-start(f32[6,2,16,384]{3,2,1,0:T(8,128)S(1)} %get-tuple-element.133), channel_id=1, source_target_pairs={{16,0},{32,16},{48,32},{64,48},{80,64},{96,80},{112,96},{17,1},{33... | collective-permute-start | bytes 884744 | tf_op jit(solution)/shard_map/ppermute | solution.py:24
  161.3 18.9 %copy-start.3 = (f32[6,32,16,384]{3,2,1,0:T(8,128)S(1)}, f32[6,32,16,384]{3,2,1,0:T(8,128)}, u32[]{:S(2)}) copy-start(f32[6,32,16,384]{3,2,1,0:T(8,128)} %scatter.31) | copy-start | bytes 14155780
  161.3 10.0 %collective-permute-start.9 = (f32[6,2,16,384]{3,2,1,0:T(8,128)S(1)}, f32[6,2,16,384]{3,2,1,0:T(8,128)S(1)}, u32[]{:S(2)}, u32[]{:S(2)}) collective-permute-start(f32[6,2,16,384]{3,2,1,0:T(8,128)S(1)} %get-tuple-element.132), channel_id=1, source_target_pairs={{0,16},{16,32},{32,48},{48,64},{64,80},{80,96},{96,112},{1,17},{17... | collective-permute-start | bytes 884744 | tf_op jit(solution)/shard_map/ppermute | solution.py:22
  174.1 11.7 %collective-permute-start.10 = (f32[6,36,2,384]{3,2,1,0:T(2,128)S(1)}, f32[6,36,2,384]{3,2,1,0:T(2,128)S(1)}, u32[]{:S(2)}, u32[]{:S(2)}) collective-permute-start(f32[6,36,2,384]{3,2,1,0:T(2,128)S(1)} %get-tuple-element.124), channel_id=1, source_target_pairs={{0,1},{1,2},{2,3},{3,4},{4,5},{5,6},{6,7},{7,8},{8,9},{9,10},{10,1... | collective-permute-start | bytes 1990664 | tf_op jit(solution)/shard_map/ppermute | solution.py:22
  178.2 14.1 %collective-permute-start.11 = (f32[6,36,2,384]{3,2,1,0:T(2,128)S(1)}, f32[6,36,2,384]{3,2,1,0:T(2,128)S(1)}, u32[]{:S(2)}, u32[]{:S(2)}) collective-permute-start(f32[6,36,2,384]{3,2,1,0:T(2,128)S(1)} %get-tuple-element.125), channel_id=1, source_target_pairs={{1,0},{2,1},{3,2},{4,3},{5,4},{6,5},{7,6},{8,7},{9,8},{10,9},{11,1... | collective-permute-start | bytes 1990664 | tf_op jit(solution)/shard_map/ppermute | solution.py:24
  197.3 63.6 %copy-start.5 = (f32[3,32,16,384]{3,2,1,0:T(8,128)S(1)}, f32[3,32,16,384]{3,2,1,0:T(8,128)}, u32[]{:S(2)}) copy-start(f32[3,32,16,384]{3,2,1,0:T(8,128)} %copy-done.4) | copy-start | bytes 7077892
  238.3 35.8 %copy-start.22 = (f32[2,384]{1,0:T(2,128)}, f32[2,384]{1,0:T(2,128)S(1)}, u32[]{:S(2)}) copy-start(f32[2,384]{1,0:T(2,128)S(1)} %get-tuple-element.105) | copy-start | bytes 9220
  260.9 33.4 %copy-start.6 = (f32[3,32,16,384]{3,2,1,0:T(8,128)}, f32[3,32,16,384]{3,2,1,0:T(8,128)S(1)}, u32[]{:S(2)}) copy-start(f32[3,32,16,384]{3,2,1,0:T(8,128)S(1)} %constant_dynamic-update-slice_fusion.7) | copy-start | bytes 7077892
  261.0 8.7 %collective-permute-start.12 = (f32[3,2,16,384]{3,2,1,0:T(8,128)S(1)}, f32[3,2,16,384]{3,2,1,0:T(8,128)S(1)}, u32[]{:S(2)}, u32[]{:S(2)}) collective-permute-start(f32[3,2,16,384]{3,2,1,0:T(8,128)S(1)} %get-tuple-element.154), channel_id=1, source_target_pairs={{0,16},{16,32},{32,48},{48,64},{64,80},{80,96},{96,112},{1,17},{17... | collective-permute-start | bytes 442376 | tf_op jit(solution)/shard_map/ppermute | solution.py:22
  264.6 9.3 %collective-permute-start.13 = (f32[3,2,16,384]{3,2,1,0:T(8,128)S(1)}, f32[3,2,16,384]{3,2,1,0:T(8,128)S(1)}, u32[]{:S(2)}, u32[]{:S(2)}) collective-permute-start(f32[3,2,16,384]{3,2,1,0:T(8,128)S(1)} %get-tuple-element.155), channel_id=1, source_target_pairs={{16,0},{32,16},{48,32},{64,48},{80,64},{96,80},{112,96},{17,1},{33... | collective-permute-start | bytes 442376 | tf_op jit(solution)/shard_map/ppermute | solution.py:24
  274.1 11.5 %collective-permute-start.14 = (f32[3,36,2,384]{3,2,1,0:T(2,128)S(1)}, f32[3,36,2,384]{3,2,1,0:T(2,128)S(1)}, u32[]{:S(2)}, u32[]{:S(2)}) collective-permute-start(f32[3,36,2,384]{3,2,1,0:T(2,128)S(1)} %get-tuple-element.149), channel_id=1, source_target_pairs={{0,1},{1,2},{2,3},{3,4},{4,5},{5,6},{6,7},{7,8},{8,9},{9,10},{10,1... | collective-permute-start | bytes 995336 | tf_op jit(solution)/shard_map/ppermute | solution.py:22
  281.6 10.5 %collective-permute-start.15 = (f32[3,36,2,384]{3,2,1,0:T(2,128)S(1)}, f32[3,36,2,384]{3,2,1,0:T(2,128)S(1)}, u32[]{:S(2)}, u32[]{:S(2)}) collective-permute-start(f32[3,36,2,384]{3,2,1,0:T(2,128)S(1)} %get-tuple-element.150), channel_id=1, source_target_pairs={{1,0},{2,1},{3,2},{4,3},{5,4},{6,5},{7,6},{8,7},{9,8},{10,9},{11,1... | collective-permute-start | bytes 995336 | tf_op jit(solution)/shard_map/ppermute | solution.py:24
  (17 other events, 46.3 us)
Sparse Core Ops, SparseCore 0:
  58.1 34.8 all-gather.4
  199.2 36.4 all-gather.6
